TPU v7x, 512 devices: a whole 4x8x8 slice. The times are simulated.
512 devices in a mesh: node: 128 (over z, y, core), feat: 4 (over x).
Axes of the slice: x: 4, y: 8, z: 8, core: 2. Of those that a mesh axis runs over, the one named last changes fastest.
Arguments:
- embed: bfloat16 [256, 131072], P('feat', 'node'), may hold values from -6 to 6
- tile_weight: bfloat16 [128, 135, 128, 128], P('node'), may hold values from -0.125 to 0.125
- tile_rows: int32 [128, 135], P('node'), may hold values from 0 to 7
- tile_cols: int32 [128, 135], P('node'), may hold values from 0 to 135, as said below
- send_rows: int32 [128, 128], P('node'), may hold values from 0 to 7
- src_local: int32 [65536], P('node'), may hold values from 0 to 1023
- dst_owner: int32 [65536, 1], P('node'), may hold values from 0 to 127; in each aligned block of 512 rows (0 to 511, 512 to 1023, ...) at most 8 rows name the same one
- dst_local: int32 [65536], P('node'), may hold values from 0 to 1023
- w_in: bfloat16 [256, 1024], P('feat'), may hold values from -0.375 to 0.375
- b_in: float32 [1024], replicated, may hold values from -4 to 4
- w_out: float32 [1024], replicated, may hold values from -0.1875 to 0.1875
Outputs:
- propagated: bfloat16 [256, 131072], P('feat', 'node')
- scores: float32 [65536], P('node')
Inputs may be any that keep to these rules, and one draw needn't show every extreme that they name: In each part, the entries of tile_cols below 8 are the numbers 0 to 7 once each, and tile_rows equals tile_cols at those tiles; the other 127 entries are 8 + p for every part p other than the part itself, once each. `dst_owner`: among the 512 queries of one part, at most 8 have the same destination part, and exactly 8 do for some destination part.
All inputs are finite; a program needn't handle non-finite values.
Results may differ from a plain program's by a relative error of at most 0.015.
Values may be sent and summed in bfloat16 or wider, within the bound.
A program may use at most 64 MiB of HBM per device.

v0:
```python
import jax
import jax.numpy as jnp
from jax import lax
from jax.sharding import PartitionSpec as P

HOPS = 2
TELEPORT = 0.1


def propagate(current, initial, weights, tile_row, tile_col, targets):
    channels, node_count = current.shape
    block_size = weights.shape[-1]
    block_count = node_count // block_size
    blocked = current.reshape(channels, block_count, block_size)
    outgoing = blocked[:, targets, :]
    incoming = lax.all_to_all(outgoing, "node", split_axis=1, concat_axis=1, tiled=True)
    sources = jnp.concatenate([blocked, incoming], axis=1)
    picked = sources[:, tile_col, :]
    products = jnp.einsum("ctj,tij->cti", picked, weights, preferred_element_type=jnp.float32)
    selector = (tile_row[None, :] == jnp.arange(block_count, dtype=jnp.int32)[:, None]).astype(
        jnp.float32
    )
    summed = jnp.einsum("rt,cti->cri", selector, products, precision=lax.Precision.HIGHEST)
    return ((1.0 - TELEPORT) * summed.reshape(channels, node_count) + TELEPORT * initial).astype(
        jnp.bfloat16
    )


def contract_rows(left_matrix, right_matrix):
    return lax.dot_general(
        left_matrix, right_matrix, (((0,), (0,)), ((), ())), preferred_element_type=jnp.float32
    )


def shards(
    embed,
    tile_weight,
    tile_rows,
    tile_cols,
    send_rows,
    src_local,
    dst_owner,
    dst_local,
    w_in,
    b_in,
    w_out,
):
    weights = tile_weight[0]
    tile_row = tile_rows[0]
    tile_col = tile_cols[0]
    targets = send_rows[0]
    initial = embed.astype(jnp.float32)
    current = embed
    for hop_index in range(HOPS):
        current = propagate(current, initial, weights, tile_row, tile_col, targets)
    part_count = lax.axis_size("node")
    queries = src_local.shape[0]
    capacity = max(2, 2 * queries // part_count)
    owners = dst_owner[:, 0]
    owner_hits = (owners[:, None] == jnp.arange(part_count, dtype=jnp.int32)[None, :]).astype(
        jnp.int32
    )
    slot_rank = jnp.sum(jnp.cumsum(owner_hits, axis=0) * owner_hits, axis=1) - 1
    requests = (
        jnp.zeros((part_count * capacity,), jnp.int32)
        .at[owners * capacity + slot_rank]
        .set(dst_local)
    )
    requests = requests.reshape(part_count, capacity)
    replies = lax.all_to_all(
        current[:, lax.all_to_all(requests, "node", split_axis=0, concat_axis=0, tiled=True)],
        "node",
        split_axis=1,
        concat_axis=1,
        tiled=True,
    )
    target_rows = replies[:, owners, slot_rank]
    source_rows = current[:, src_local]
    hadamard = (source_rows.astype(jnp.float32) * target_rows.astype(jnp.float32)).astype(
        jnp.bfloat16
    )
    partial_value = contract_rows(w_in, hadamard)
    hidden = lax.psum(partial_value.astype(jnp.bfloat16), "feat").astype(jnp.float32)
    active = jnp.maximum(hidden + b_in[:, None], 0.0)
    scores = jnp.dot(w_out, active, precision=lax.Precision.HIGHEST)
    return (current, scores)


def solution(mesh):
    placed = (
        P("feat", "node"),
        P("node", None, None, None),
        P("node", None),
        P("node", None),
        P("node", None),
        P("node"),
        P("node", None),
        P("node"),
        P("feat", None),
        P(),
        P(),
    )
    return jax.shard_map(
        shards,
        mesh=mesh,
        in_specs=placed,
        out_specs=(P("feat", "node"), P("node")),
        check_vma=False,
    )
```

profile of v0, /device:TPU:8, one launch (start us, length us, event | category | flops | bytes accessed | tf_op | source)
XLA Modules:
  0.0 273.8 jit_solution(4774526276266268185)
XLA Ops:
  7.2 1.0 copy_bitcast_fusion
  8.1 0.7 fusion.56
  8.8 2.2 gather_fusion
  11.0 17.5 %all-to-all-start = ((bf16[64,128,128]{2,0,1:T(8,128)(2,1)}), bf16[64,128,128]{2,0,1:T(8,128)(2,1)S(1)}, u32[]{:S(2)}, u32[]{:S(2)}) async-start(bf16[64,128,128]{2,0,1:T(8,128)(2,1)} %bitcast.90), calls=%async_computation | async-start | bytes 4194304 | tf_op jit(solution)/shard_map/all_to_all | solution.py:16
  29.1 0.2 fusion.41
  29.4 2.6 scatter_custom_fusion
  32.0 0.7 all_to_all.19
  32.7 49.8 %all-to-all-done = bf16[64,128,128]{2,0,1:T(8,128)(2,1)S(1)} async-done(((bf16[64,128,128]{2,0,1:T(8,128)(2,1)}), bf16[64,128,128]{2,0,1:T(8,128)(2,1)S(1)}, u32[]{:S(2)}, u32[]{:S(2)}) %all-to-all-start) | async-done | bytes 2097184 | tf_op jit(solution)/shard_map/all_to_all | solution.py:16
  82.5 6.1 %all-to-all-start.2 = ((s32[128,1,8]{2,1,0:T(1,128)}), s32[128,1,8]{2,1,0:T(1,128)S(1)}, u32[]{:S(2)}, u32[]{:S(2)}) async-start(s32[128,1,8]{2,1,0:T(1,128)} %bitcast.25), calls=%async_computation.2 | async-start | bytes 131072 | tf_op jit(solution)/shard_map/all_to_all | solution.py:71
  88.6 1.6 pad_maximum_fusion
  90.2 2.6 gather_fusion.1
  92.8 5.4 %fusion.10 = f32[64,135,128]{2,0,1:T(8,128)S(1)} fusion(bf16[1,135,128,128]{3,2,1,0:T(8,128)(2,1)} %param.12, bf16[135,64,128]{2,1,0:T(8,128)(2,1)S(1)} %gather_fusion.1), kind=kOutput, calls=%fused_computation.20 | convolution fusion | flops 283115520 | bytes 11059200 | tf_op jit(solution)/shard_map/ctj,tij->cti/dot_general | solution.py:19
  98.2 4.0 %fusion.34 = f32[64,8,128]{2,1,0:T(8,128)S(1)} fusion(f32[64,135,128]{2,0,1:T(8,128)S(1)} %fusion.10, s32[135]{0:T(256)S(1)} %bitcast.101), kind=kOutput, calls=%fused_computation.31 | convolution fusion | flops 106234936 | bytes 4686364 | tf_op jit(solution)/shard_map/rt,cti->cri/dot_general | solution.py:23
  102.2 0.2 copy.83
  102.7 2.2 gather_fusion.2
  104.8 13.7 %all-to-all-start.1 = ((bf16[64,128,128]{2,0,1:T(8,128)(2,1)}), bf16[64,128,128]{2,0,1:T(8,128)(2,1)S(1)}, u32[]{:S(2)}, u32[]{:S(2)}) async-start(bf16[64,128,128]{2,0,1:T(8,128)(2,1)} %bitcast.13), calls=%async_computation.1 | async-start | bytes 4194304 | tf_op jit(solution)/shard_map/all_to_all | solution.py:16
  118.7 53.9 %all-to-all-done.1 = bf16[64,128,128]{2,0,1:T(8,128)(2,1)S(1)} async-done(((bf16[64,128,128]{2,0,1:T(8,128)(2,1)}), bf16[64,128,128]{2,0,1:T(8,128)(2,1)S(1)}, u32[]{:S(2)}, u32[]{:S(2)}) %all-to-all-start.1) | async-done | bytes 2097184 | tf_op jit(solution)/shard_map/all_to_all | solution.py:16
  172.6 1.6 pad_maximum_fusion.1
  174.2 2.6 gather_fusion.3
  176.8 5.4 %fusion.15 = f32[64,135,128]{2,0,1:T(8,128)S(1)} fusion(bf16[1,135,128,128]{3,2,1,0:T(8,128)(2,1)} %param.12, bf16[135,64,128]{2,1,0:T(8,128)(2,1)S(1)} %gather_fusion.3), kind=kOutput, calls=%fused_computation.21 | convolution fusion | flops 283115520 | bytes 11059200 | tf_op jit(solution)/shard_map/ctj,tij->cti/dot_general | solution.py:19
  182.2 4.0 %fusion.31 = f32[64,8,128]{2,1,0:T(8,128)S(1)} fusion(f32[64,135,128]{2,0,1:T(8,128)S(1)} %fusion.15, s32[135]{0:T(256)S(1)} %bitcast.102), kind=kOutput, calls=%fused_computation.30 | convolution fusion | flops 106234936 | bytes 4686364 | tf_op jit(solution)/shard_map/rt,cti->cri/dot_general | solution.py:23
  186.5 3.2 %gather_fusion.5 = bf16[1024,64]{1,0:T(8,128)(2,1)S(1)} fusion(bf16[64,1024]{0,1:T(8,128)(2,1)S(1)} %fusion.39, s32[1024]{0:T(1024)S(1)} %broadcast_clamp_fusion), kind=kCustom, calls=%fused_computation.5 | custom fusion | bytes 266240 | tf_op jit(solution)/shard_map/gather | solution.py:71
  189.8 0.9 reshape.217
  190.7 6.2 %all-to-all-start.3 = ((bf16[128,2,256]{2,1,0:T(2,128)(2,1)}), bf16[128,2,256]{2,1,0:T(2,128)(2,1)S(1)}, u32[]{:S(2)}, u32[]{:S(2)}) async-start(bf16[128,2,256]{2,1,0:T(2,128)(2,1)} %reshape.217), calls=%async_computation.3 | async-start | bytes 262144 | tf_op jit(solution)/shard_map/all_to_all | solution.py:70
  196.8 0.3 all-reduce.2.cloned.1.call-start
  197.2 1.3 gather_fusion.4
  198.6 10.2 %all-to-all-done.3 = bf16[128,2,256]{2,1,0:T(2,128)(2,1)S(1)} async-done(((bf16[128,2,256]{2,1,0:T(2,128)(2,1)}), bf16[128,2,256]{2,1,0:T(2,128)(2,1)S(1)}, u32[]{:S(2)}, u32[]{:S(2)}) %all-to-all-start.3) | async-done | bytes 131104 | tf_op jit(solution)/shard_map/all_to_all | solution.py:70
  209.0 3.1 %gather_fusion.6 = bf16[512,64]{1,0:T(8,128)(2,1)S(1)} fusion(bf16[64,128,8]{0,2,1:T(8,128)(2,1)S(1)} %bitcast.91, s32[512]{0:T(512)S(1)} %bitcast.89), kind=kCustom, calls=%fused_computation.6 | custom fusion | bytes 135168 | tf_op jit(solution)/shard_map/gather | solution.py:77
  212.1 1.5 fusion.24
  213.6 0.8 copy.82
  214.4 48.7 %all-reduce.2.cloned.1.call-done = bf16[1024,512]{0,1:T(8,128)(2,1)} async-done(((bf16[1024,512]{0,1:T(8,128)(2,1)}), bf16[1024,512]{0,1:T(8,128)(2,1)}) %all-reduce.2.cloned.1.call-update) | async-done | bytes 1048592 | tf_op jit(solution)/shard_map/psum | solution.py:83
  263.1 3.9 %fusion.20 = f32[1,512]{1,0:T(1,128)} fusion(f32[1024,1]{0,1:T(1,128)S(1)} %bitcast.105, bf16[1024,512]{0,1:T(8,128)(2,1)} %all-reduce.2.cloned.1.call-done, f32[1024]{0:T(1024)S(1)} %copy-done.7), kind=kOutput, calls=%fused_computation.22 | convolution fusion | flops 7864320 | bytes 1058816 | tf_op jit(solution)/shard_map/dot_general | solution.py:85
  (43 shorter events, 1.5 us)
Async XLA Ops:
  7.2 204.9 %copy-start = (bf16[64,1024]{1,0:T(8,128)(2,1)S(1)}, bf16[64,1024]{1,0:T(8,128)(2,1)}, u32[]{:S(2)}) copy-start(bf16[64,1024]{1,0:T(8,128)(2,1)} %param.19) | copy-start | bytes 393220
  11.0 17.5 %copy-start.1 = (bf16[64,1024]{1,0:T(8,128)(2,1)S(1)}, bf16[64,1024]{1,0:T(8,128)(2,1)}, u32[]{:S(2)}) copy-start(bf16[64,1024]{1,0:T(8,128)(2,1)} %param.11) | copy-start | bytes 393220
  11.0 17.7 %copy-start.2 = (s32[512,1]{0,1:T(1,128)S(1)}, s32[512,1]{0,1:T(1,128)}, u32[]{:S(2)}) copy-start(s32[512,1]{0,1:T(1,128)} %param.17) | copy-start | bytes 6148
  11.0 21.7 %copy-start.5 = (s32[1,135]{1,0:T(1,128)S(1)}, s32[1,135]{1,0:T(1,128)}, u32[]{:S(2)}) copy-start(s32[1,135]{1,0:T(1,128)} %param.14) | copy-start | bytes 1624
  11.0 71.6 %all-to-all-start = ((bf16[64,128,128]{2,0,1:T(8,128)(2,1)}), bf16[64,128,128]{2,0,1:T(8,128)(2,1)S(1)}, u32[]{:S(2)}, u32[]{:S(2)}) async-start(bf16[64,128,128]{2,0,1:T(8,128)(2,1)} %bitcast.90), calls=%async_computation | async-start | bytes 4194304 | tf_op jit(solution)/shard_map/all_to_all | solution.py:16
  82.5 22.3 %all-to-all-start.2 = ((s32[128,1,8]{2,1,0:T(1,128)}), s32[128,1,8]{2,1,0:T(1,128)S(1)}, u32[]{:S(2)}, u32[]{:S(2)}) async-start(s32[128,1,8]{2,1,0:T(1,128)} %bitcast.25), calls=%async_computation.2 | async-start | bytes 131072 | tf_op jit(solution)/shard_map/all_to_all | solution.py:71
  92.8 5.4 %copy-start.3 = (s32[1,135]{1,0:T(1,128)S(1)}, s32[1,135]{1,0:T(1,128)}, u32[]{:S(2)}) copy-start(s32[1,135]{1,0:T(1,128)} %param.13) | copy-start | bytes 1624
  104.8 67.8 %all-to-all-start.1 = ((bf16[64,128,128]{2,0,1:T(8,128)(2,1)}), bf16[64,128,128]{2,0,1:T(8,128)(2,1)S(1)}, u32[]{:S(2)}, u32[]{:S(2)}) async-start(bf16[64,128,128]{2,0,1:T(8,128)(2,1)} %bitcast.13), calls=%async_computation.1 | async-start | bytes 4194304 | tf_op jit(solution)/shard_map/all_to_all | solution.py:16
  186.5 10.6 %copy-start.4 = (s32[512]{0:T(512)S(1)}, s32[512]{0:T(512)}, u32[]{:S(2)}) copy-start(s32[512]{0:T(512)} %param.16) | copy-start | bytes 6148
  190.7 18.1 %all-to-all-start.3 = ((bf16[128,2,256]{2,1,0:T(2,128)(2,1)}), bf16[128,2,256]{2,1,0:T(2,128)(2,1)S(1)}, u32[]{:S(2)}, u32[]{:S(2)}) async-start(bf16[128,2,256]{2,1,0:T(2,128)(2,1)} %reshape.217), calls=%async_computation.3 | async-start | bytes 262144 | tf_op jit(solution)/shard_map/all_to_all | solution.py:70
  196.8 66.2 %all-reduce.2.cloned.1.call-start = ((), (), s32[]{:S(2)}) async-start(), calls=%async_computation.4 | async-start | bytes 2097152 | tf_op jit(solution)/shard_map/psum | solution.py:83
  198.5 64.6 %copy-start.6 = (f32[1024]{0:T(1024)S(1)}, f32[1024]{0:T(1024)}, u32[]{:S(2)}) copy-start(f32[1024]{0:T(1024)} %param.21) | copy-start | bytes 12292
  198.5 64.5 %copy-start.7 = (f32[1024]{0:T(1024)S(1)}, f32[1024]{0:T(1024)}, u32[]{:S(2)}) copy-start(f32[1024]{0:T(1024)} %param.20) | copy-start | bytes 12292
Sparse Core Ops, SparseCore 0:
  213.7 49.3 all-reduce.1
where the time goes:
time: 274 us
  waiting for transfers between devices  163 us (59%)
  starting transfers between devices  43.8 us (16%)
  local copies, waits for them, and re-layouts  24.4 us (9%)
  matrix products  24.1 us (9%)
  between operations  14.3 us (5%)
  other arithmetic  4.5 us (2%)
    all_to_all x2, waiting for transfers between devices, propagate(): lax.all_to_all(outgoing, 'node', split_axis=1, concat_axis=1, tiled=True)  104 us
    psum x1, waiting for transfers between devices, shards(): lax.psum(partial_value.astype(jnp.bfloat16), 'feat').astype(jnp.float32)  48.7 us
    all_to_all x2, starting transfers between devices, propagate(): lax.all_to_all(outgoing, 'node', split_axis=1, concat_axis=1, tiled=True)  31.2 us
    dot_general x2, matrix products, propagate(): jnp.einsum('ctj,tij->cti', picked, weights, preferred_element_type=jnp.fl...  10.8 us
    all_to_all x1, waiting for transfers between devices, shards(): lax.all_to_all(current[:, lax.all_to_all(requests, 'node', split_axis=0,...  10.2 us
    dot_general x2, matrix products, propagate(): jnp.einsum('rt,cti->cri', selector, products, precision=lax.Precision.HIG...  7.96 us
    all_to_all x1, starting transfers between devices, shards(): lax.all_to_all(current[:, lax.all_to_all(requests, 'node', split_axis=0,...  6.16 us
    all_to_all x1, starting transfers between devices, shards(): lax.all_to_all(requests, 'node', split_axis=0, concat_axis=0, tiled=True)  6.07 us
  transfers between devices with their start and end apart: 5, of which 4 were waited for; matrix products, arithmetic and copies ran while one was open for 8% of the time, Pallas kernels for 0%

commit v1 on v0

--- a/solution.py
+++ b/solution.py
@@ -67,12 +67,14 @@
         .set(dst_local)
     )
     requests = requests.reshape(part_count, capacity)
-    replies = lax.all_to_all(
-        current[:, lax.all_to_all(requests, "node", split_axis=0, concat_axis=0, tiled=True)],
-        "node",
-        split_axis=1,
-        concat_axis=1,
-        tiled=True,
+
+    def compute_the_loops(t0):
+        return jnp.concatenate(
+            lax.all_to_all(jnp.stack(jnp.split(t0, lax.axis_size("node"), 1)), "node", 0, 0), axis=1
+        )
+
+    replies = compute_the_loops(
+        current[:, lax.all_to_all(requests, "node", split_axis=0, concat_axis=0, tiled=True)]
     )
     target_rows = replies[:, owners, slot_rank]
     source_rows = current[:, src_local]

time: 274 us -> 277 us (1.011)
  no operation moved by 1% of the time
where the time goes in v1:
time: 277 us; the launch traced here: 276 us
  waiting for transfers between devices  163 us (59%)
  starting transfers between devices  43.8 us (16%)
  local copies, waits for them, and re-layouts  25.4 us (9%)
  matrix products  24.1 us (9%)
  between operations  14.7 us (5%)
  other arithmetic  5.21 us (2%)
    all_to_all x2, waiting for transfers between devices, propagate(): lax.all_to_all(outgoing, 'node', split_axis=1, concat_axis=1, tiled=True)  104 us
    psum x1, waiting for transfers between devices, shards(): lax.psum(partial_value.astype(jnp.bfloat16), 'feat').astype(jnp.float32)  48.7 us
    all_to_all x2, starting transfers between devices, propagate(): lax.all_to_all(outgoing, 'node', split_axis=1, concat_axis=1, tiled=True)  31.2 us
    dot_general x2, matrix products, propagate(): jnp.einsum('ctj,tij->cti', picked, weights, preferred_element_type=jnp.fl...  10.8 us
    all_to_all x1, waiting for transfers between devices, compute_the_loops(): lax.all_to_all(jnp.stack(jnp.split(t0, lax.axis_size('node'), 1)), 'node'...  10.3 us
    dot_general x2, matrix products, propagate(): jnp.einsum('rt,cti->cri', selector, products, precision=lax.Precision.HIG...  7.96 us
    all_to_all x1, starting transfers between devices, compute_the_loops(): lax.all_to_all(jnp.stack(jnp.split(t0, lax.axis_size('node'), 1)), 'node'...  6.16 us
    all_to_all x1, starting transfers between devices, shards(): lax.all_to_all(requests, 'node', split_axis=0, concat_axis=0, tiled=True)  6.07 us
  transfers between devices with their start and end apart: 5, of which 4 were waited for; matrix products, arithmetic and copies ran while one was open for 8% of the time, Pallas kernels for 0%

profile of v1, /device:TPU:8, one launch (start us, length us, event | category | flops | bytes accessed | tf_op | source)
XLA Modules:
  0.0 276.0 jit_solution(10958176911067411110)
XLA Ops:
  7.2 0.7 compare_select_fusion.5
  7.9 0.7 fusion.56
  8.6 0.9 copy_bitcast_fusion
  9.5 2.2 gather_fusion
  11.7 17.5 %all-to-all-start = ((bf16[64,128,128]{2,0,1:T(8,128)(2,1)}), bf16[64,128,128]{2,0,1:T(8,128)(2,1)S(1)}, u32[]{:S(2)}, u32[]{:S(2)}) async-start(bf16[64,128,128]{2,0,1:T(8,128)(2,1)} %bitcast.735), calls=%async_computation | async-start | bytes 4194304 | tf_op jit(solution)/shard_map/all_to_all | solution.py:16
  29.8 0.2 fusion.41
  30.1 2.6 scatter_custom_fusion
  32.7 0.7 all_to_all.19
  33.4 49.8 %all-to-all-done = bf16[64,128,128]{2,0,1:T(8,128)(2,1)S(1)} async-done(((bf16[64,128,128]{2,0,1:T(8,128)(2,1)}), bf16[64,128,128]{2,0,1:T(8,128)(2,1)S(1)}, u32[]{:S(2)}, u32[]{:S(2)}) %all-to-all-start) | async-done | bytes 2097184 | tf_op jit(solution)/shard_map/all_to_all | solution.py:16
  83.2 6.1 %all-to-all-start.2 = ((s32[128,1,8]{2,1,0:T(1,128)}), s32[128,1,8]{2,1,0:T(1,128)S(1)}, u32[]{:S(2)}, u32[]{:S(2)}) async-start(s32[128,1,8]{2,1,0:T(1,128)} %bitcast.25), calls=%async_computation.2 | async-start | bytes 131072 | tf_op jit(solution)/shard_map/all_to_all | solution.py:77
  89.3 1.6 pad_maximum_fusion
  90.9 2.6 gather_fusion.1
  93.5 5.4 %fusion.10 = f32[64,135,128]{2,0,1:T(8,128)S(1)} fusion(bf16[1,135,128,128]{3,2,1,0:T(8,128)(2,1)} %param.12, bf16[135,64,128]{2,1,0:T(8,128)(2,1)S(1)} %gather_fusion.1), kind=kOutput, calls=%fused_computation.20 | convolution fusion | flops 283115520 | bytes 11059200 | tf_op jit(solution)/shard_map/ctj,tij->cti/dot_general | solution.py:19
  98.9 4.0 %fusion.34 = f32[64,8,128]{2,1,0:T(8,128)S(1)} fusion(f32[64,135,128]{2,0,1:T(8,128)S(1)} %fusion.10, s32[135]{0:T(256)S(1)} %bitcast.746), kind=kOutput, calls=%fused_computation.31 | convolution fusion | flops 106234936 | bytes 4686364 | tf_op jit(solution)/shard_map/rt,cti->cri/dot_general | solution.py:23
  103.4 2.2 gather_fusion.2
  105.5 13.7 %all-to-all-start.1 = ((bf16[64,128,128]{2,0,1:T(8,128)(2,1)}), bf16[64,128,128]{2,0,1:T(8,128)(2,1)S(1)}, u32[]{:S(2)}, u32[]{:S(2)}) async-start(bf16[64,128,128]{2,0,1:T(8,128)(2,1)} %bitcast.13), calls=%async_computation.1 | async-start | bytes 4194304 | tf_op jit(solution)/shard_map/all_to_all | solution.py:16
  119.4 53.9 %all-to-all-done.1 = bf16[64,128,128]{2,0,1:T(8,128)(2,1)S(1)} async-done(((bf16[64,128,128]{2,0,1:T(8,128)(2,1)}), bf16[64,128,128]{2,0,1:T(8,128)(2,1)S(1)}, u32[]{:S(2)}, u32[]{:S(2)}) %all-to-all-start.1) | async-done | bytes 2097184 | tf_op jit(solution)/shard_map/all_to_all | solution.py:16
  173.3 1.6 pad_maximum_fusion.1
  174.9 2.6 gather_fusion.3
  177.5 5.4 %fusion.15 = f32[64,135,128]{2,0,1:T(8,128)S(1)} fusion(bf16[1,135,128,128]{3,2,1,0:T(8,128)(2,1)} %param.12, bf16[135,64,128]{2,1,0:T(8,128)(2,1)S(1)} %gather_fusion.3), kind=kOutput, calls=%fused_computation.21 | convolution fusion | flops 283115520 | bytes 11059200 | tf_op jit(solution)/shard_map/ctj,tij->cti/dot_general | solution.py:19
  182.9 4.0 %fusion.31 = f32[64,8,128]{2,1,0:T(8,128)S(1)} fusion(f32[64,135,128]{2,0,1:T(8,128)S(1)} %fusion.15, s32[135]{0:T(256)S(1)} %bitcast.747), kind=kOutput, calls=%fused_computation.30 | convolution fusion | flops 106234936 | bytes 4686364 | tf_op jit(solution)/shard_map/rt,cti->cri/dot_general | solution.py:23
  187.2 3.2 %gather_fusion.5 = bf16[1024,64]{1,0:T(8,128)(2,1)S(1)} fusion(bf16[64,1024]{0,1:T(8,128)(2,1)S(1)} %fusion.39, s32[1024]{0:T(1024)S(1)} %broadcast_clamp_fusion), kind=kCustom, calls=%fused_computation.5 | custom fusion | bytes 266240 | tf_op jit(solution)/shard_map/gather | solution.py:77
  192.0 0.9 reshape.225
  192.9 6.2 %all-to-all-start.3 = ((bf16[128,2,256]{2,1,0:T(2,128)(2,1)}), bf16[128,2,256]{2,1,0:T(2,128)(2,1)S(1)}, u32[]{:S(2)}, u32[]{:S(2)}) async-start(bf16[128,2,256]{2,1,0:T(2,128)(2,1)} %reshape.225), calls=%async_computation.3 | async-start | bytes 262144 | tf_op jit(solution)/shard_map/all_to_all | solution.py:73
  199.0 0.3 all-reduce.2.cloned.1.call-start
  199.3 1.3 gather_fusion.4
  200.7 10.3 %all-to-all-done.3 = bf16[128,2,256]{2,1,0:T(2,128)(2,1)S(1)} async-done(((bf16[128,2,256]{2,1,0:T(2,128)(2,1)}), bf16[128,2,256]{2,1,0:T(2,128)(2,1)S(1)}, u32[]{:S(2)}, u32[]{:S(2)}) %all-to-all-start.3) | async-done | bytes 131104 | tf_op jit(solution)/shard_map/all_to_all | solution.py:73
  211.3 3.1 %gather_fusion.6 = bf16[512,64]{1,0:T(8,128)(2,1)S(1)} fusion(bf16[64,128,8]{0,2,1:T(8,128)(2,1)S(1)} %bitcast_bitcast_fusion, s32[512]{0:T(512)S(1)} %bitcast.606), kind=kCustom, calls=%fused_computation.6 | custom fusion | bytes 135168 | tf_op jit(solution)/shard_map/gather | solution.py:79
  214.3 1.5 fusion.24
  215.8 0.8 copy.845
  216.6 48.7 %all-reduce.2.cloned.1.call-done = bf16[1024,512]{0,1:T(8,128)(2,1)} async-done(((bf16[1024,512]{0,1:T(8,128)(2,1)}), bf16[1024,512]{0,1:T(8,128)(2,1)}) %all-reduce.2.cloned.1.call-update) | async-done | bytes 1048592 | tf_op jit(solution)/shard_map/psum | solution.py:85
  265.3 3.9 %fusion.20 = f32[1,512]{1,0:T(1,128)} fusion(f32[1024,1]{0,1:T(1,128)S(1)} %bitcast.750, bf16[1024,512]{0,1:T(8,128)(2,1)} %all-reduce.2.cloned.1.call-done, f32[1024]{0:T(1024)S(1)} %copy-done.6), kind=kOutput, calls=%fused_computation.22 | convolution fusion | flops 7864320 | bytes 1058816 | tf_op jit(solution)/shard_map/dot_general | solution.py:87
  (168 shorter events, 2.9 us)
Async XLA Ops:
  7.2 207.2 %copy-start = (bf16[64,1024]{1,0:T(8,128)(2,1)S(1)}, bf16[64,1024]{1,0:T(8,128)(2,1)}, u32[]{:S(2)}) copy-start(bf16[64,1024]{1,0:T(8,128)(2,1)} %param.19) | copy-start | bytes 393220
  11.7 17.5 %copy-start.1 = (bf16[64,1024]{1,0:T(8,128)(2,1)S(1)}, bf16[64,1024]{1,0:T(8,128)(2,1)}, u32[]{:S(2)}) copy-start(bf16[64,1024]{1,0:T(8,128)(2,1)} %param.11) | copy-start | bytes 393220
  11.7 17.7 %copy-start.2 = (s32[512,1]{0,1:T(1,128)S(1)}, s32[512,1]{0,1:T(1,128)}, u32[]{:S(2)}) copy-start(s32[512,1]{0,1:T(1,128)} %param.17) | copy-start | bytes 6148
  11.7 21.7 %copy-start.4 = (s32[1,135]{1,0:T(1,128)S(1)}, s32[1,135]{1,0:T(1,128)}, u32[]{:S(2)}) copy-start(s32[1,135]{1,0:T(1,128)} %param.14) | copy-start | bytes 1624
  11.7 71.6 %all-to-all-start = ((bf16[64,128,128]{2,0,1:T(8,128)(2,1)}), bf16[64,128,128]{2,0,1:T(8,128)(2,1)S(1)}, u32[]{:S(2)}, u32[]{:S(2)}) async-start(bf16[64,128,128]{2,0,1:T(8,128)(2,1)} %bitcast.735), calls=%async_computation | async-start | bytes 4194304 | tf_op jit(solution)/shard_map/all_to_all | solution.py:16
  83.2 22.3 %all-to-all-start.2 = ((s32[128,1,8]{2,1,0:T(1,128)}), s32[128,1,8]{2,1,0:T(1,128)S(1)}, u32[]{:S(2)}, u32[]{:S(2)}) async-start(s32[128,1,8]{2,1,0:T(1,128)} %bitcast.25), calls=%async_computation.2 | async-start | bytes 131072 | tf_op jit(solution)/shard_map/all_to_all | solution.py:77
  93.5 5.4 %copy-start.3 = (s32[1,135]{1,0:T(1,128)S(1)}, s32[1,135]{1,0:T(1,128)}, u32[]{:S(2)}) copy-start(s32[1,135]{1,0:T(1,128)} %param.13) | copy-start | bytes 1624
  105.5 67.8 %all-to-all-start.1 = ((bf16[64,128,128]{2,0,1:T(8,128)(2,1)}), bf16[64,128,128]{2,0,1:T(8,128)(2,1)S(1)}, u32[]{:S(2)}, u32[]{:S(2)}) async-start(bf16[64,128,128]{2,0,1:T(8,128)(2,1)} %bitcast.13), calls=%async_computation.1 | async-start | bytes 4194304 | tf_op jit(solution)/shard_map/all_to_all | solution.py:16
  192.9 18.1 %all-to-all-start.3 = ((bf16[128,2,256]{2,1,0:T(2,128)(2,1)}), bf16[128,2,256]{2,1,0:T(2,128)(2,1)S(1)}, u32[]{:S(2)}, u32[]{:S(2)}) async-start(bf16[128,2,256]{2,1,0:T(2,128)(2,1)} %reshape.225), calls=%async_computation.3 | async-start | bytes 262144 | tf_op jit(solution)/shard_map/all_to_all | solution.py:73
  199.0 66.3 %all-reduce.2.cloned.1.call-start = ((), (), s32[]{:S(2)}) async-start(), calls=%async_computation.4 | async-start | bytes 2097152 | tf_op jit(solution)/shard_map/psum | solution.py:85
  211.2 54.1 %copy-start.5 = (f32[1024]{0:T(1024)S(1)}, f32[1024]{0:T(1024)}, u32[]{:S(2)}) copy-start(f32[1024]{0:T(1024)} %param.21) | copy-start | bytes 12292
  211.2 54.1 %copy-start.6 = (f32[1024]{0:T(1024)S(1)}, f32[1024]{0:T(1024)}, u32[]{:S(2)}) copy-start(f32[1024]{0:T(1024)} %param.20) | copy-start | bytes 12292
Sparse Core Ops, SparseCore 0:
  215.9 49.3 all-reduce.1
